TPU v7x, 128 devices: a whole 4x4x4 slice. The times are simulated.
128 devices in a mesh: front: 4 (over z), tile: 32 (over x, y, core).
Axes of the slice: x: 4, y: 4, z: 4, core: 2. Of those that a mesh axis runs over, the one named last changes fastest.
Arguments:
- front_entries: float32 [4, 4096, 4096], P('front', 'tile')
- child_blocks: bfloat16 [512, 64, 256], P(('front', 'tile'))
- child_map: int32 [128, 256], replicated, may hold values from -1 to 4095, as said below
- parent_list: int32 [128, 1], replicated, may hold values from 0 to 3; in each aligned block of 4 rows (0 to 3, 4 to 7, ...) at most 2 rows name the same one
Outputs:
- front_out: float32 [4, 4096, 4096], P('front', 'tile')
Inputs may be any that keep to these rules, and one draw needn't show every extreme that they name: `child_map`: row c gives the parent-front row of each of the 256 rows of child c: live entries come first and are distinct, -1 marks padding, every row has 128 to 256 live entries, and its first entry is 4095. `parent_list`: in each aligned block of 4 rows no front is named more than 2 times.
All inputs are finite; a program needn't handle non-finite values.
Results may differ from a plain program's by a relative error of at most 0.0003.
Values may be sent and summed in bfloat16 or wider, within the bound.
A program may use at most 128 MiB of HBM per device.

v0:
```python
import jax
import jax.numpy as jnp
from jax import lax
from jax.sharding import PartitionSpec as P

FRONT = 4096
PANEL = 512
PANELS = 2
CHILD = 256
BLOCK_ROWS = 64
BLK_DEV = 4
CAPACITY = 2


def routing(child_map, parent_list, front_count, tile_count, group_id):
    child_count = child_map.shape[0]
    fronts = jnp.arange(front_count, dtype=jnp.int32)
    target = parent_list[:, 0]
    blocks = (
        jnp.arange(front_count * tile_count, dtype=jnp.int32)[:, None] * BLK_DEV
        + jnp.arange(BLK_DEV, dtype=jnp.int32)[None, :]
    )
    child_of = blocks % child_count
    part_of = blocks // child_count
    child_ids = jnp.arange(child_count, dtype=jnp.int32)
    dest_front = jnp.sum(jnp.where(child_of[..., None] == child_ids, target, 0), axis=2)
    earlier = jnp.arange(BLK_DEV)[:, None] > jnp.arange(BLK_DEV)[None, :]
    same_dest = dest_front[:, :, None] == dest_front[:, None, :]
    slot_rank = jnp.sum(same_dest & earlier[None], axis=2)
    slot_ids = jnp.arange(CAPACITY, dtype=jnp.int32)
    select = (dest_front[:, None, None, :] == fronts[None, :, None, None]) & (
        slot_rank[:, None, None, :] == slot_ids[None, None, :, None]
    )
    to_group = select[:, group_id]
    slot_live = jnp.any(to_group, axis=2)
    slot_child = jnp.sum(jnp.where(to_group, child_of[:, None, :], 0), axis=2)
    slot_part = jnp.sum(jnp.where(to_group, part_of[:, None, :], 0), axis=2)
    return (select, slot_live, slot_child, slot_part)


def body(front_entries, child_blocks, child_map, parent_list):
    tile_count = lax.axis_size("tile")
    front_count = lax.axis_size("front")
    group_id = lax.axis_index("front")
    tile_id = lax.axis_index("tile")
    rows_dev = front_entries.shape[1]
    first_row = tile_id * rows_dev
    child_count = child_map.shape[0]
    select, slot_live, slot_child, slot_part = routing(
        child_map, parent_list, front_count, tile_count, group_id
    )
    self_dev = group_id * tile_count + tile_id
    own_select = select[self_dev].astype(jnp.bfloat16)
    outgoing = jnp.einsum(
        "dsj,jrk->dsrk", own_select, child_blocks, preferred_element_type=jnp.float32
    ).astype(jnp.bfloat16)
    incoming = lax.all_to_all(outgoing, "front", split_axis=0, concat_axis=0, tiled=True)
    child_hot = (slot_child[..., None] == jnp.arange(child_count, dtype=jnp.int32)).astype(
        jnp.float32
    )
    map_values = jnp.einsum(
        "dsn,nk->dsk", child_hot, child_map.astype(jnp.float32), precision=lax.Precision.HIGHEST
    )
    col_flat = map_values.astype(jnp.int32)
    part_count = CHILD // BLOCK_ROWS
    col_parts = col_flat.reshape(col_flat.shape[0], CAPACITY, part_count, BLOCK_ROWS)
    part_hot = slot_part[..., None] == jnp.arange(part_count, dtype=jnp.int32)
    row_maps = jnp.sum(jnp.where(part_hot[..., None], col_parts, 0), axis=2)
    row_valid = slot_live[..., None] & (row_maps >= 0)
    row_table = jnp.where(row_valid, row_maps, FRONT).reshape(
        front_count, tile_count, CAPACITY, BLOCK_ROWS
    )
    col_table = col_flat.reshape(front_count, tile_count, CAPACITY, CHILD)
    empty_cols = jnp.zeros((FRONT, rows_dev), jnp.float32)
    front_ids = jnp.arange(FRONT, dtype=jnp.int32)
    own_columns = first_row + jnp.arange(rows_dev)
    shards = lax.all_gather(incoming[None], "tile", axis=0, tiled=True)

    def one_tile(tile_step, running):
        child_rows = lax.dynamic_index_in_dim(shards, tile_step, 0, keepdims=False)
        col_maps = lax.dynamic_index_in_dim(col_table, tile_step, 1, keepdims=False)
        matches = (col_maps[..., None] == own_columns[None, None, None, :]).astype(jnp.bfloat16)
        values = jnp.einsum(
            "gsrk,gskc->gsrc", child_rows, matches, preferred_element_type=jnp.float32
        ).astype(jnp.bfloat16)
        targets = lax.dynamic_index_in_dim(row_table, tile_step, 1, keepdims=False)
        row_hot = (targets[..., None] == front_ids).astype(jnp.bfloat16)
        return running + jnp.einsum(
            "gsrf,gsrc->fc", row_hot, values, preferred_element_type=jnp.float32
        )

    extend_cols = lax.fori_loop(0, shards.shape[0], one_tile, empty_cols)
    matrix = front_entries[0] + extend_cols.T
    row_ids = first_row + jnp.arange(rows_dev)
    for panel_no in range(PANELS):
        left_col = panel_no * PANEL
        right_col = left_col + PANEL
        cols_piece = matrix[:, left_col:right_col]
        gathered = lax.all_gather(
            cols_piece.astype(jnp.bfloat16), "tile", axis=0, tiled=True
        ).astype(cols_piece.dtype)
        diag_factor = jnp.linalg.cholesky(gathered[left_col:right_col])
        lower_part = jax.scipy.linalg.solve_triangular(
            diag_factor, gathered[right_col:].T, lower=True
        ).T
        factor = jnp.concatenate([diag_factor, lower_part], 0)
        slice_start = jnp.clip(first_row - left_col, 0, FRONT - left_col - rows_dev)
        own_rows = lax.dynamic_slice_in_dim(factor, slice_start, rows_dev, 0)
        trailing = jnp.where((row_ids >= right_col)[:, None], own_rows, 0.0)
        remainder = matrix[:, right_col:] - jnp.dot(
            trailing, lower_part.T, precision=lax.Precision.HIGHEST
        )
        in_lower = row_ids[:, None] - left_col >= jnp.arange(PANEL)[None, :]
        panel_out = jnp.where(in_lower, own_rows, cols_piece)
        matrix = jnp.concatenate([matrix[:, :left_col], panel_out, remainder], 1)
    return matrix[None]


def solution(mesh):
    return jax.shard_map(
        body,
        mesh=mesh,
        in_specs=(P("front", "tile", None), P(("front", "tile"), None, None), P(), P()),
        out_specs=P("front", "tile", None),
        check_vma=False,
    )
```

profile of v0, /device:TPU:1, one launch (start us, length us, event | category | flops | bytes accessed | tf_op | source)
XLA Modules:
  0.0 746.4 jit_solution(17177670713988524720)
XLA Ops:
  11.6 11.3 %all_to_all.5 = bf16[4,2,64,256]{3,2,1,0:T(8,128)(2,1)} all-to-all(bf16[4,2,64,256]{3,2,1,0:T(8,128)(2,1)S(1)} %copy.98), channel_id=1, replica_groups=mesh['front'=4,'tile'=32] {'front'}, dimensions={0} | all-to-all | bytes 524288 | tf_op jit(solution)/shard_map/all_to_all | solution.py:57
  30.5 46.6 %all-gather.9.cloned.1.call-done = bf16[128,2,64,256]{3,2,1,0:T(8,128)(2,1)} async-done(((bf16[4,2,64,256]{3,2,1,0:T(8,128)(2,1)}), bf16[128,2,64,256]{3,2,1,0:T(8,128)(2,1)}) %all-gather.9.cloned.1.call-update) | async-done | bytes 8388624 | tf_op jit(solution)/shard_map/all_gather | solution.py:77
  77.2 186.3 %while.18 = (s32[]{:T(128)}, f32[4096,128]{1,0:T(8,128)}, s32[4,32,2,64]{3,1,0,2:T(8,128)S(1)}, bf16[32,4,2,64,256]{4,3,2,1,0:T(8,128)(2,1)}, s32[4,32,2,256]{3,...) while((s32[]{:T(128)}, f32[4096,128]{1,0:T(8,128)}, s32[4,32,2,64]{3,1,0,2:T(8,128)S(1)}, ...), condition=%wide.region_7.8_spmd.clone, body=%wide.region_6.7_spmd.clone.sunk | while | flops 573898880 | bytes 4508791 | solution.py:92
  82.4 5.8 fusion.141
  94.1 5.8 fusion.141
  105.7 5.8 fusion.141
  111.6 5.8 fusion.141
  117.4 5.8 fusion.141
  123.3 5.8 fusion.141
  129.1 5.8 fusion.141
  267.6 48.6 %all-gather.5.cloned.1.call-done = bf16[4096,512]{0,1:T(8,128)(2,1)} async-done(((bf16[128,512]{0,1:T(8,128)(2,1)}), bf16[4096,512]{0,1:T(8,128)(2,1)}) %all-gather.5.cloned.1.call-update) | async-done | bytes 4194320 | tf_op jit(solution)/shard_map/all_gather | solution.py:99
  324.8 11.7 %cholesky.286 = f32[128,128]{1,0:T(8,128)S(1)} custom-call(f32[128,128]{1,0:T(8,128)S(1)} %cholesky.426), custom_call_target="Cholesky" | custom-call | tf_op jit(solution)/shard_map/jit(cholesky)/cholesky | solution.py:102
  336.7 9.8 %custom-call.34 = f32[1,128,128]{1,2,0:T(8,128)S(1)} custom-call(f32[1,128,128]{2,1,0:T(8,128)S(1)} %get-tuple-element.280), custom_call_target="InvertDiagBlocksLowerTriangular" | custom-call | tf_op jit(solution)/shard_map/jit(cholesky)/cholesky | solution.py:102
  347.3 12.1 %cholesky.305 = f32[128,128]{1,0:T(8,128)S(1)} custom-call(f32[128,128]{1,0:T(8,128)S(1)} %cholesky.430), custom_call_target="Cholesky" | custom-call | tf_op jit(solution)/shard_map/jit(cholesky)/cholesky | solution.py:102
  359.6 9.8 %custom-call.35 = f32[1,128,128]{1,2,0:T(8,128)S(1)} custom-call(f32[1,128,128]{2,1,0:T(8,128)S(1)} %get-tuple-element.278), custom_call_target="InvertDiagBlocksLowerTriangular" | custom-call | tf_op jit(solution)/shard_map/jit(cholesky)/cholesky | solution.py:102
  374.4 11.7 %cholesky.326 = f32[128,128]{1,0:T(8,128)S(1)} custom-call(f32[128,128]{1,0:T(8,128)S(1)} %cholesky.435), custom_call_target="Cholesky" | custom-call | tf_op jit(solution)/shard_map/jit(cholesky)/cholesky | solution.py:102
  386.9 9.8 %custom-call.36 = f32[1,128,128]{1,2,0:T(8,128)S(1)} custom-call(f32[1,128,128]{2,1,0:T(8,128)S(1)} %get-tuple-element.276), custom_call_target="InvertDiagBlocksLowerTriangular" | custom-call | tf_op jit(solution)/shard_map/jit(cholesky)/cholesky | solution.py:102
  399.1 11.9 %cholesky.343 = f32[128,128]{1,0:T(8,128)S(1)} custom-call(f32[128,128]{1,0:T(8,128)S(1)} %convolution_subtract_fusion.11), custom_call_target="Cholesky" | custom-call | tf_op jit(solution)/shard_map/jit(cholesky)/cholesky | solution.py:102
  419.5 11.4 %while.16 = (s32[]{:T(128)}, f32[512,512]{0,1:T(8,128)}, s32[4,2]{0,1:T(2,128)S(1)}, f32[4,128,128]{2,1,0:T(8,128)S(1)}, s32[]{:T(128)}) while((s32[]{:T(128)}, f32[512,512]{0,1:T(8,128)}, s32[4,2]{0,1:T(2,128)S(1)}, f32[4,128,128]{2,1,0:T(8,128)S(1)}, s32[]{:T(128)}) %tuple.89), condition=%wide.while_cond, body=%wide.while_body.sunk | while | flops 2 | bytes 393329 | solution.py:103
  431.6 40.1 %custom-call.28 = f32[4,128,128]{1,2,0:T(8,128)S(1)} custom-call(f32[4,128,128]{2,1,0:T(8,128)} %copy-done.8), custom_call_target="InvertDiagBlocksLowerTriangular" | custom-call | tf_op jit(solution)/shard_map/jit(_solve_triangular)/triangular_solve | solution.py:103
  493.7 12.4 %convolution_subtract_fusion = f32[128,3584]{0,1:T(8,128)S(1)} fusion(f32[128,3584]{1,0:T(8,128)S(1)} %fusion.90, f32[128,3584]{1,0:T(8,128)S(1)} %fusion.91, f32[128,3584]{1,0:T(8,128)S(1)} %fusion.93, f32[128,3584]{1,0:T(8,128)S(1)} %fusion.50, f32[128,4096]{0,1:T(8,128)S(1)} %copy-done.3, pred[128]{0:T(512)(128)(4,1)S(1)} %broadcast_compare_fusion.1, ...), kind=kOutput, calls=%fused_computation.37 | convolution fusion | flops 2824667136 | bytes 19398788 | tf_op jit(solution)/shard_map/dot_general | solution.py:110
  508.2 48.6 %all-gather.7.cloned.1.call-done = bf16[4096,512]{0,1:T(8,128)(2,1)} async-done(((bf16[128,512]{0,1:T(8,128)(2,1)}), bf16[4096,512]{0,1:T(8,128)(2,1)}) %all-gather.7.cloned.1.call-update) | async-done | bytes 4194320 | tf_op jit(solution)/shard_map/all_gather | solution.py:99
  564.9 11.7 %cholesky.358 = f32[128,128]{1,0:T(8,128)S(1)} custom-call(f32[128,128]{1,0:T(8,128)S(1)} %cholesky.439), custom_call_target="Cholesky" | custom-call | tf_op jit(solution)/shard_map/jit(cholesky)/cholesky | solution.py:102
  576.8 9.8 %custom-call.37 = f32[1,128,128]{1,2,0:T(8,128)S(1)} custom-call(f32[1,128,128]{2,1,0:T(8,128)S(1)} %get-tuple-element.274), custom_call_target="InvertDiagBlocksLowerTriangular" | custom-call | tf_op jit(solution)/shard_map/jit(cholesky)/cholesky | solution.py:102
  587.4 12.1 %cholesky.377 = f32[128,128]{1,0:T(8,128)S(1)} custom-call(f32[128,128]{1,0:T(8,128)S(1)} %cholesky.443), custom_call_target="Cholesky" | custom-call | tf_op jit(solution)/shard_map/jit(cholesky)/cholesky | solution.py:102
  599.6 9.8 %custom-call.38 = f32[1,128,128]{1,2,0:T(8,128)S(1)} custom-call(f32[1,128,128]{2,1,0:T(8,128)S(1)} %get-tuple-element.272), custom_call_target="InvertDiagBlocksLowerTriangular" | custom-call | tf_op jit(solution)/shard_map/jit(cholesky)/cholesky | solution.py:102
  610.5 11.7 %cholesky.398 = f32[128,128]{1,0:T(8,128)S(1)} custom-call(f32[128,128]{1,0:T(8,128)S(1)} %cholesky.448), custom_call_target="Cholesky" | custom-call | tf_op jit(solution)/shard_map/jit(cholesky)/cholesky | solution.py:102
  622.4 9.8 %custom-call.39 = f32[1,128,128]{1,2,0:T(8,128)S(1)} custom-call(f32[1,128,128]{2,1,0:T(8,128)S(1)} %get-tuple-element.270), custom_call_target="InvertDiagBlocksLowerTriangular" | custom-call | tf_op jit(solution)/shard_map/jit(cholesky)/cholesky | solution.py:102
  633.0 11.9 %cholesky.415 = f32[128,128]{1,0:T(8,128)S(1)} custom-call(f32[128,128]{1,0:T(8,128)S(1)} %convolution_subtract_fusion.10), custom_call_target="Cholesky" | custom-call | tf_op jit(solution)/shard_map/jit(cholesky)/cholesky | solution.py:102
  653.5 14.5 %while.17 = (s32[]{:T(128)}, f32[512,512]{0,1:T(8,128)}, s32[4,2]{0,1:T(2,128)S(1)}, f32[4,128,128]{2,1,0:T(8,128)}, s32[]{:T(128)}) while((s32[]{:T(128)}, f32[512,512]{0,1:T(8,128)}, s32[4,2]{0,1:T(2,128)S(1)}, f32[4,128,128]{2,1,0:T(8,128)}, s32[]{:T(128)}) %tuple.102), condition=%wide.while_cond.1, body=%wide.while_body.1.sunk | while | flops 2 | bytes 393329 | solution.py:103
  668.0 40.7 %custom-call.29 = f32[4,128,128]{1,2,0:T(8,128)} custom-call(f32[4,128,128]{2,1,0:T(8,128)} %get-tuple-element.146), custom_call_target="InvertDiagBlocksLowerTriangular" | custom-call | tf_op jit(solution)/shard_map/jit(_solve_triangular)/triangular_solve | solution.py:103
  726.9 10.5 %convolution_subtract_fusion.4 = f32[128,3072]{0,1:T(8,128)S(1)} fusion(f32[128,3072]{1,0:T(8,128)S(1)} %fusion.84, f32[128,3072]{1,0:T(8,128)S(1)} %fusion.85, f32[128,3072]{1,0:T(8,128)S(1)} %fusion.87, f32[128,3072]{1,0:T(8,128)S(1)} %fusion.52, f32[128,3584]{0,1:T(8,128)S(1)} %copy-done.5, pred[128]{0:T(512)(128)(4,1)S(1)} %broadcast_compare_fusion, ...), kind=kOutput, calls=%fused_computation.49 | convolution fusion | flops 2421161984 | bytes 16777348 | tf_op jit(solution)/shard_map/dot_general | solution.py:110
  (381 shorter events, 273.1 us)
Async XLA Ops:
  6.5 21.4 %copy-start.9 = (s32[128,256]{1,0:T(8,128)S(1)}, s32[128,256]{1,0:T(8,128)}, u32[]{:S(2)}) copy-start(s32[128,256]{1,0:T(8,128)} %param.9) | copy-start | bytes 393220
  6.5 70.7 %all-gather.9.cloned.1.call-start = ((), (), s32[]{:S(2)}) async-start(), calls=%async_computation.3 | async-start | bytes 8650752 | tf_op jit(solution)/shard_map/all_gather | solution.py:77
  22.9 293.2 %all-gather.5.cloned.1.call-start = ((), (), s32[]{:S(2)}) async-start(), calls=%async_computation.1 | async-start | bytes 4325376 | tf_op jit(solution)/shard_map/all_gather | solution.py:99
  265.3 1.3 copy-start.2
  267.3 289.5 %all-gather.7.cloned.1.call-start = ((), (), s32[]{:S(2)}) async-start(), calls=%async_computation.2 | async-start | bytes 4325376 | tf_op jit(solution)/shard_map/all_gather | solution.py:99
  416.4 58.7 %slice-start = ((s8[7340032]{0:T(1024)(128)(4,1)}), s8[3145728]{0:T(1024)(128)(4,1)S(1)}, s32[]{:S(2)}) async-start(s8[7340032]{0:T(1024)(128)(4,1)} %bitcast.155), calls=%async_computation.4 | async-start | bytes 6291456
  430.9 0.7 copy-start.8
  471.7 3.4 slice-start.1
  490.8 1.2 copy-start.1
  490.8 2.8 copy-start.3
  491.4 14.7 %copy-start = (f32[3584,512]{0,1:T(8,128)}, f32[3584,512]{0,1:T(8,128)S(1)}, u32[]{:S(2)}) copy-start(f32[3584,512]{0,1:T(8,128)S(1)} %fusion.35) | copy-start | bytes 22020100
  506.0 1.2 copy-start.4
  647.6 1.9 copy-start.6
  650.1 61.7 %slice-start.2 = ((s8[6291456]{0:T(1024)(128)(4,1)}), s8[2097152]{0:T(1024)(128)(4,1)S(1)}, s32[]{:S(2)}) async-start(s8[6291456]{0:T(1024)(128)(4,1)} %bitcast.157), calls=%async_computation.6 | async-start | bytes 4194304
  708.7 2.3 copy-start.7
  708.7 3.2 slice-start.3
  725.4 1.5 copy-start.5
Sparse Core Ops, SparseCore 0:
  23.1 54.0 all-gather.8
  267.4 48.7 all-gather.4
  508.1 48.6 all-gather.6
where the time goes:
time: 756 us; the launch traced here: 746 us
  other arithmetic  265 us (35%)
  matrix products  247 us (33%)
  waiting for transfers between devices  144 us (19%)
  local copies, waits for them, and re-layouts  58.7 us (8%)
  between operations  19.3 us (3%)
  blocking collectives  11.3 us (1%)
    dot_general x32, matrix products, one_tile(): jnp.einsum('gsrf,gsrc->fc', row_hot, values, preferred_element_type=jnp.f...  184 us
    another operation x29, other arithmetic, body(): diag_factor = jnp.linalg.cholesky(gathered[left_col:right_col])  159 us
    all_gather x2, waiting for transfers between devices, body(): lax.all_gather(cols_piece.astype(jnp.bfloat16), 'tile', axis=0, tiled=True)  97.2 us
    another operation x5, other arithmetic, body(): jax.scipy.linalg.solve_triangular(diag_factor, gathered[right_col:].T, lo...  86.6 us
    all_gather x1, waiting for transfers between devices, body(): shards = lax.all_gather(incoming[None], 'tile', axis=0, tiled=True)  46.6 us
    another operation x14, matrix products, body(): jax.scipy.linalg.solve_triangular(diag_factor, gathered[right_col:].T, lo...  30.7 us
    another operation x40, local copies, waits for them, and re-layouts  25.7 us
    dot_general x2, matrix products, body(): jnp.dot(trailing, lower_part.T, precision=lax.Precision.HIGHEST)  22.8 us
  transfers between devices with their start and end apart: 3, of which 3 were waited for; matrix products, arithmetic and copies ran while one was open for 1% of the time, Pallas kernels for 0%

commit v1 on v0

--- a/solution.py
+++ b/solution.py
@@ -74,7 +74,9 @@
     empty_cols = jnp.zeros((FRONT, rows_dev), jnp.float32)
     front_ids = jnp.arange(FRONT, dtype=jnp.int32)
     own_columns = first_row + jnp.arange(rows_dev)
-    shards = lax.all_gather(incoming[None], "tile", axis=0, tiled=True)
+    part = incoming[None]
+    stack = jnp.stack([part] * lax.axis_size("tile"))
+    shards = jnp.concatenate(lax.all_to_all(stack, "tile", 0, 0), axis=0)
 
     def one_tile(tile_step, running):
         child_rows = lax.dynamic_index_in_dim(shards, tile_step, 0, keepdims=False)

time: 756 us -> 846 us (1.12)
  waiting for transfers between devices: 144 us -> 212 us
  local copies, waits for them, and re-layouts: 58.7 us -> 72.9 us
  starting transfers between devices: 0.3 us -> 9.65 us
    all_to_all x0 -> x1, waiting for transfers between devices: none -> 101 us  [body(): shards = jnp.concatenate(lax.all_to_all(stack, 'tile', 0, 0), axis=0)]
    all_gather x1 -> x0, waiting for transfers between devices: 46.6 us -> none  [body(): shards = lax.all_gather(incoming[None], 'tile', axis=0, tiled=True)]
    all_gather x2, waiting for transfers between devices: 97.2 us -> 111 us  [body(): lax.all_gather(cols_piece.astype(jnp.bfloat16), 'tile', axis=0, tiled=True)]
    all_to_all x0 -> x1, starting transfers between devices: none -> 9.35 us  [body(): shards = jnp.concatenate(lax.all_to_all(stack, 'tile', 0, 0), axis=0)]
    another operation x40 -> x41, local copies, waits for them, and re-layouts: 25.7 us -> 30.5 us
where the time goes in v1:
time: 846 us; the launch traced here: 835 us
  other arithmetic  264 us (31%)
  matrix products  244 us (29%)
  waiting for transfers between devices  212 us (25%)
  local copies, waits for them, and re-layouts  72.9 us (9%)
  between operations  19.7 us (2%)
  blocking collectives  11.2 us (1%)
  starting transfers between devices  9.65 us (1%)
    dot_general x32, matrix products, one_tile(): jnp.einsum('gsrf,gsrc->fc', row_hot, values, preferred_element_type=jnp.f...  184 us
    another operation x29, other arithmetic, body(): diag_factor = jnp.linalg.cholesky(gathered[left_col:right_col])  158 us
    all_gather x2, waiting for transfers between devices, body(): lax.all_gather(cols_piece.astype(jnp.bfloat16), 'tile', axis=0, tiled=True)  111 us
    all_to_all x1, waiting for transfers between devices, body(): shards = jnp.concatenate(lax.all_to_all(stack, 'tile', 0, 0), axis=0)  101 us
    another operation x5, other arithmetic, body(): jax.scipy.linalg.solve_triangular(diag_factor, gathered[right_col:].T, lo...  86.5 us
    another operation x14, matrix products, body(): jax.scipy.linalg.solve_triangular(diag_factor, gathered[right_col:].T, lo...  30.7 us
    another operation x40, local copies, waits for them, and re-layouts  26.2 us
    dot_general x2, matrix products, body(): jnp.dot(trailing, lower_part.T, precision=lax.Precision.HIGHEST)  22.8 us
  transfers between devices with their start and end apart: 3, of which 3 were waited for; matrix products, arithmetic and copies ran while one was open for 1% of the time, Pallas kernels for 0%

profile of v1, /device:TPU:1, one launch (start us, length us, event | category | flops | bytes accessed | tf_op | source)
XLA Modules:
  0.0 835.2 jit_solution(9615403740856751535)
XLA Ops:
  11.5 11.2 %all_to_all.10 = bf16[4,2,64,256]{3,2,1,0:T(8,128)(2,1)S(1)} all-to-all(bf16[4,2,64,256]{3,2,1,0:T(8,128)(2,1)S(1)} %copy.98), channel_id=1, replica_groups=mesh['front'=4,'tile'=32] {'front'}, dimensions={0} | all-to-all | bytes 524288 | tf_op jit(solution)/shard_map/all_to_all | solution.py:57
  27.0 9.3 %all-to-all-start.1 = ((bf16[32,1,4,2,64,256]{5,4,3,2,1,0:T(8,128)(2,1)}), bf16[32,1,4,2,64,256]{5,4,3,2,1,0:T(8,128)(2,1)}, u32[]{:S(2)}, u32[]{:S(2)}) async-start(bf16[32,1,4,2,64,256]{5,4,3,2,1,0:T(8,128)(2,1)} %stack.3), calls=%async_computation.1 | async-start | bytes 16777216 | tf_op jit(solution)/shard_map/all_to_all | solution.py:79
  44.0 100.9 %all-to-all-done.1 = bf16[32,1,4,2,64,256]{5,4,3,2,1,0:T(8,128)(2,1)} async-done(((bf16[32,1,4,2,64,256]{5,4,3,2,1,0:T(8,128)(2,1)}), bf16[32,1,4,2,64,256]{5,4,3,2,1,0:T(8,128)(2,1)}, u32[]{:S(2)}, u32[]{:S(2)}) %all-to-all-start.1) | async-done | bytes 8388640 | tf_op jit(solution)/shard_map/all_to_all | solution.py:79
  144.9 186.7 %while.18 = (s32[]{:T(128)}, f32[4096,128]{1,0:T(8,128)}, s32[4,32,2,64]{3,1,0,2:T(8,128)S(1)}, bf16[32,4,2,64,256]{4,3,2,1,0:T(8,128)(2,1)}, s32[4,32,2,256]{3,...) while((s32[]{:T(128)}, f32[4096,128]{1,0:T(8,128)}, s32[4,32,2,64]{3,1,0,2:T(8,128)S(1)}, ...), condition=%wide.region_7.8_spmd.clone, body=%wide.region_6.7_spmd.clone.sunk | while | flops 573898880 | bytes 4509291 | solution.py:94
  150.1 5.8 fusion.141
  179.4 5.8 fusion.141
  185.3 5.8 fusion.141
  191.1 5.8 fusion.141
  335.7 62.6 %all-gather.3.cloned.1.call-done = bf16[4096,512]{0,1:T(8,128)(2,1)} async-done(((bf16[128,512]{0,1:T(8,128)(2,1)}), bf16[4096,512]{0,1:T(8,128)(2,1)}) %all-gather.3.cloned.1.call-update) | async-done | bytes 4194320 | tf_op jit(solution)/shard_map/all_gather | solution.py:101
  406.5 11.7 %cholesky.286 = f32[128,128]{1,0:T(8,128)S(1)} custom-call(f32[128,128]{1,0:T(8,128)S(1)} %cholesky.426), custom_call_target="Cholesky" | custom-call | tf_op jit(solution)/shard_map/jit(cholesky)/cholesky | solution.py:104
  418.3 9.8 %custom-call.34 = f32[1,128,128]{1,2,0:T(8,128)S(1)} custom-call(f32[1,128,128]{2,1,0:T(8,128)S(1)} %get-tuple-element.280), custom_call_target="InvertDiagBlocksLowerTriangular" | custom-call | tf_op jit(solution)/shard_map/jit(cholesky)/cholesky | solution.py:104
  428.8 11.7 %cholesky.305 = f32[128,128]{1,0:T(8,128)S(1)} custom-call(f32[128,128]{1,0:T(8,128)S(1)} %cholesky.430), custom_call_target="Cholesky" | custom-call | tf_op jit(solution)/shard_map/jit(cholesky)/cholesky | solution.py:104
  440.9 10.2 %custom-call.35 = f32[1,128,128]{1,2,0:T(8,128)S(1)} custom-call(f32[1,128,128]{2,1,0:T(8,128)S(1)} %get-tuple-element.278), custom_call_target="InvertDiagBlocksLowerTriangular" | custom-call | tf_op jit(solution)/shard_map/jit(cholesky)/cholesky | solution.py:104
  452.2 11.7 %cholesky.326 = f32[128,128]{1,0:T(8,128)S(1)} custom-call(f32[128,128]{1,0:T(8,128)S(1)} %cholesky.435), custom_call_target="Cholesky" | custom-call | tf_op jit(solution)/shard_map/jit(cholesky)/cholesky | solution.py:104
  464.1 9.8 %custom-call.36 = f32[1,128,128]{1,2,0:T(8,128)S(1)} custom-call(f32[1,128,128]{2,1,0:T(8,128)S(1)} %get-tuple-element.276), custom_call_target="InvertDiagBlocksLowerTriangular" | custom-call | tf_op jit(solution)/shard_map/jit(cholesky)/cholesky | solution.py:104
  474.7 11.9 %cholesky.343 = f32[128,128]{1,0:T(8,128)S(1)} custom-call(f32[128,128]{1,0:T(8,128)S(1)} %convolution_subtract_fusion.11), custom_call_target="Cholesky" | custom-call | tf_op jit(solution)/shard_map/jit(cholesky)/cholesky | solution.py:104
  486.7 6.6 slice_bitcast_fusion
  501.0 12.2 %while.16 = (s32[]{:T(128)}, f32[512,512]{0,1:T(8,128)}, s32[4,2]{0,1:T(2,128)S(1)}, f32[4,128,128]{2,1,0:T(8,128)S(1)}, s32[]{:T(128)}) while((s32[]{:T(128)}, f32[512,512]{0,1:T(8,128)}, s32[4,2]{0,1:T(2,128)S(1)}, f32[4,128,128]{2,1,0:T(8,128)S(1)}, s32[]{:T(128)}) %tuple.89), condition=%wide.while_cond, body=%wide.while_body.sunk | while | flops 2 | bytes 393321 | solution.py:105
  513.8 40.1 %custom-call.28 = f32[4,128,128]{1,2,0:T(8,128)S(1)} custom-call(f32[4,128,128]{2,1,0:T(8,128)} %copy-done.11), custom_call_target="InvertDiagBlocksLowerTriangular" | custom-call | tf_op jit(solution)/shard_map/jit(_solve_triangular)/triangular_solve | solution.py:105
  575.9 12.4 %convolution_subtract_fusion = f32[128,3584]{0,1:T(8,128)S(1)} fusion(f32[128,3584]{1,0:T(8,128)S(1)} %fusion.90, f32[128,3584]{1,0:T(8,128)S(1)} %fusion.91, f32[128,3584]{1,0:T(8,128)S(1)} %fusion.93, f32[128,3584]{1,0:T(8,128)S(1)} %fusion.50, f32[128,4096]{0,1:T(8,128)S(1)} %copy-done.5, pred[128]{0:T(512)(128)(4,1)S(1)} %broadcast_compare_fusion.1, ...), kind=kOutput, calls=%fused_computation.37 | convolution fusion | flops 2824667136 | bytes 19398788 | tf_op jit(solution)/shard_map/dot_general | solution.py:112
  590.5 48.6 %all-gather.5.cloned.1.call-done = bf16[4096,512]{0,1:T(8,128)(2,1)} async-done(((bf16[128,512]{0,1:T(8,128)(2,1)}), bf16[4096,512]{0,1:T(8,128)(2,1)}) %all-gather.5.cloned.1.call-update) | async-done | bytes 4194320 | tf_op jit(solution)/shard_map/all_gather | solution.py:101
  647.3 11.7 %cholesky.358 = f32[128,128]{1,0:T(8,128)S(1)} custom-call(f32[128,128]{1,0:T(8,128)S(1)} %cholesky.439), custom_call_target="Cholesky" | custom-call | tf_op jit(solution)/shard_map/jit(cholesky)/cholesky | solution.py:104
  659.0 9.8 %custom-call.37 = f32[1,128,128]{1,2,0:T(8,128)S(1)} custom-call(f32[1,128,128]{2,1,0:T(8,128)S(1)} %get-tuple-element.274), custom_call_target="InvertDiagBlocksLowerTriangular" | custom-call | tf_op jit(solution)/shard_map/jit(cholesky)/cholesky | solution.py:104
  669.5 11.7 %cholesky.377 = f32[128,128]{1,0:T(8,128)S(1)} custom-call(f32[128,128]{1,0:T(8,128)S(1)} %cholesky.443), custom_call_target="Cholesky" | custom-call | tf_op jit(solution)/shard_map/jit(cholesky)/cholesky | solution.py:104
  682.0 9.8 %custom-call.38 = f32[1,128,128]{1,2,0:T(8,128)S(1)} custom-call(f32[1,128,128]{2,1,0:T(8,128)S(1)} %get-tuple-element.272), custom_call_target="InvertDiagBlocksLowerTriangular" | custom-call | tf_op jit(solution)/shard_map/jit(cholesky)/cholesky | solution.py:104
  692.9 11.7 %cholesky.398 = f32[128,128]{1,0:T(8,128)S(1)} custom-call(f32[128,128]{1,0:T(8,128)S(1)} %cholesky.448), custom_call_target="Cholesky" | custom-call | tf_op jit(solution)/shard_map/jit(cholesky)/cholesky | solution.py:104
  704.8 9.8 %custom-call.39 = f32[1,128,128]{1,2,0:T(8,128)S(1)} custom-call(f32[1,128,128]{2,1,0:T(8,128)S(1)} %get-tuple-element.270), custom_call_target="InvertDiagBlocksLowerTriangular" | custom-call | tf_op jit(solution)/shard_map/jit(cholesky)/cholesky | solution.py:104
  715.4 11.9 %cholesky.415 = f32[128,128]{1,0:T(8,128)S(1)} custom-call(f32[128,128]{1,0:T(8,128)S(1)} %convolution_subtract_fusion.10), custom_call_target="Cholesky" | custom-call | tf_op jit(solution)/shard_map/jit(cholesky)/cholesky | solution.py:104
  727.4 6.2 slice_bitcast_fusion.1
  742.3 14.2 %while.17 = (s32[]{:T(128)}, f32[512,512]{0,1:T(8,128)}, s32[4,2]{0,1:T(2,128)S(1)}, f32[4,128,128]{2,1,0:T(8,128)}, s32[]{:T(128)}) while((s32[]{:T(128)}, f32[512,512]{0,1:T(8,128)}, s32[4,2]{0,1:T(2,128)S(1)}, f32[4,128,128]{2,1,0:T(8,128)}, s32[]{:T(128)}) %tuple.100), condition=%wide.while_cond.1, body=%wide.while_body.1.sunk | while | flops 2 | bytes 393829 | solution.py:105
  756.5 40.7 %custom-call.29 = f32[4,128,128]{1,2,0:T(8,128)} custom-call(f32[4,128,128]{2,1,0:T(8,128)} %get-tuple-element.146), custom_call_target="InvertDiagBlocksLowerTriangular" | custom-call | tf_op jit(solution)/shard_map/jit(_solve_triangular)/triangular_solve | solution.py:105
  815.6 10.5 %convolution_subtract_fusion.4 = f32[128,3072]{0,1:T(8,128)S(1)} fusion(f32[128,3072]{1,0:T(8,128)S(1)} %fusion.84, f32[128,3072]{1,0:T(8,128)S(1)} %fusion.85, f32[128,3072]{1,0:T(8,128)S(1)} %fusion.87, f32[128,3072]{1,0:T(8,128)S(1)} %fusion.52, f32[128,3584]{0,1:T(8,128)S(1)} %copy-done.7, pred[128]{0:T(512)(128)(4,1)S(1)} %broadcast_compare_fusion, ...), kind=kOutput, calls=%fused_computation.49 | convolution fusion | flops 2421161984 | bytes 16777348 | tf_op jit(solution)/shard_map/dot_general | solution.py:112
  (387 shorter events, 288.5 us)
Async XLA Ops:
  27.0 14.2 %copy-start.12 = (s32[128,256]{1,0:T(8,128)S(1)}, s32[128,256]{1,0:T(8,128)}, u32[]{:S(2)}) copy-start(s32[128,256]{1,0:T(8,128)} %param.9) | copy-start | bytes 393220
  27.0 117.9 %all-to-all-start.1 = ((bf16[32,1,4,2,64,256]{5,4,3,2,1,0:T(8,128)(2,1)}), bf16[32,1,4,2,64,256]{5,4,3,2,1,0:T(8,128)(2,1)}, u32[]{:S(2)}, u32[]{:S(2)}) async-start(bf16[32,1,4,2,64,256]{5,4,3,2,1,0:T(8,128)(2,1)} %stack.3), calls=%async_computation.1 | async-start | bytes 16777216 | tf_op jit(solution)/shard_map/all_to_all | solution.py:79
  36.4 361.9 %all-gather.3.cloned.1.call-start = ((), (), s32[]{:S(2)}) async-start(), calls=%async_computation.2 | async-start | bytes 4325376 | tf_op jit(solution)/shard_map/all_gather | solution.py:101
  333.4 1.3 copy-start.4
  335.4 303.6 %all-gather.5.cloned.1.call-start = ((), (), s32[]{:S(2)}) async-start(), calls=%async_computation.3 | async-start | bytes 4325376 | tf_op jit(solution)/shard_map/all_gather | solution.py:101
  403.1 3.2 copy-start.1
  494.6 2.8 copy-start.8
  497.9 59.4 %slice-start = ((s8[7340032]{0:T(1024)(128)(4,1)}), s8[3145728]{0:T(1024)(128)(4,1)S(1)}, s32[]{:S(2)}) async-start(s8[7340032]{0:T(1024)(128)(4,1)} %bitcast.155), calls=%async_computation.4 | async-start | bytes 6291456
  513.1 0.7 copy-start.11
  554.0 3.4 slice-start.1
  573.0 1.2 copy-start.3
  573.1 2.8 copy-start.5
  573.6 14.7 %copy-start = (f32[3584,512]{0,1:T(8,128)}, f32[3584,512]{0,1:T(8,128)S(1)}, u32[]{:S(2)}) copy-start(f32[3584,512]{0,1:T(8,128)S(1)} %fusion.35) | copy-start | bytes 22020100
  588.3 1.2 copy-start.6
  643.8 3.2 copy-start.2
  736.3 1.9 copy-start.9
  738.9 61.4 %slice-start.2 = ((s8[6291456]{0:T(1024)(128)(4,1)}), s8[2097152]{0:T(1024)(128)(4,1)S(1)}, s32[]{:S(2)}) async-start(s8[6291456]{0:T(1024)(128)(4,1)} %bitcast.157), calls=%async_computation.6 | async-start | bytes 4194304
  797.2 2.3 copy-start.10
  797.2 3.2 slice-start.3
  813.9 1.5 copy-start.7
Sparse Core Ops, SparseCore 0:
  335.5 62.6 all-gather.2
  590.3 48.6 all-gather.4
